TPU v7x, 32 devices: a whole 2x2x4 slice. The times are simulated.
32 devices in a mesh: boot: 2 (over x), samp: 16 (over z, y, core).
Axes of the slice: x: 2, y: 2, z: 4, core: 2. Of those that a mesh axis runs over, the one named last changes fastest.
Arguments:
- dosage: bfloat16 [32384, 512], P('samp'), may hold values from 0 to 2, as said below
- residuals: bfloat16 [32384, 1280], P('samp', 'boot'), may hold values from -300 to 300
- maf_bin: int32 [512], replicated, may hold values from 0 to 63
- gene_map: int32 [512], replicated, may hold values from 0 to 31, never falling along the last dimension, each value on 1 to 32 neighbouring positions
- gene_order: int32 [32], replicated, may hold values from 0 to 31, each once
Outputs:
- calibrated: float32 [32, 1280], P('samp', 'boot')
Inputs may be any that keep to these rules, and one draw needn't show every extreme that they name: `dosage`: allele counts 0, 1 or 2. `gene_map`: never falling along the variants; each gene holds 1 to 32 consecutive variants, one gene exactly 32. `gene_order`: each gene once.
All inputs are finite; a program needn't handle non-finite values.
Results may differ from a plain program's by a relative error of at most 0.0003.
Values sent between devices are 32-bit elements; how exact they have to be, the bound alone decides.
A program may use at most 64 MiB of HBM per device.

v0:
```python
import math
import jax
import jax.numpy as jnp
from jax import lax
from jax.sharding import PartitionSpec as P

GENE_DEV = 2
RHOS = 11
MAF_BINS = 64
EPSILON = 1e-05


def variant_weights(maf_bin):
    levels = jnp.arange(MAF_BINS, dtype=jnp.float32)
    weight_table = (1.0 - 0.05 * (levels + 0.5) / MAF_BINS) ** 24
    matches = maf_bin[:, None] == jnp.arange(MAF_BINS, dtype=jnp.int32)[None, :]
    return jnp.sum(
        jnp.where(matches, weight_table[None, :], jnp.zeros_like(weight_table)[None, :]), axis=1
    )


def sample_product(dose_part, residuals):
    return lax.dot_general(
        dose_part, residuals, (((0,), (0,)), ((), ())), preferred_element_type=jnp.float32
    )


def shards(dosage, residuals, maf_bin, gene_map, gene_order):
    sample_total = dosage.shape[0] * lax.axis_size("samp")
    scaling = variant_weights(maf_bin) / math.sqrt(sample_total)
    my_index = lax.axis_index("samp")
    partial_value = sample_product(dosage, residuals) * scaling[:, None]
    scores = lax.psum(partial_value, "samp")
    owned_genes = lax.dynamic_slice_in_dim(gene_order, my_index * GENE_DEV, GENE_DEV)
    member = (owned_genes[:, None] == gene_map[None, :]).astype(jnp.float32)
    stacked = jnp.concatenate([scores, scores * scores], axis=1)
    gene_sums = jnp.dot(
        member, stacked, precision=lax.Precision.HIGHEST, preferred_element_type=jnp.float32
    )
    boot_local = residuals.shape[1]
    burden = gene_sums[:, :boot_local]
    skat = gene_sums[:, boot_local:]
    rho_grid = jnp.arange(RHOS, dtype=jnp.float32) / (RHOS - 1)
    mixtures = (1.0 - rho_grid)[None, :, None] * skat[:, None, :] + rho_grid[None, :, None] * (
        burden * burden
    )[:, None, :]
    boot_total = boot_local * lax.axis_size("boot")
    first_sum, square_sum = lax.psum(
        (jnp.sum(mixtures, axis=2), jnp.sum(mixtures * mixtures, axis=2)), "boot"
    )
    center = first_sum / boot_total
    spread = square_sum / boot_total - center * center
    deviation = mixtures - center[:, :, None]
    zscore = deviation / jnp.sqrt(spread[:, :, None] + EPSILON)
    return jnp.max(zscore, axis=1)


def solution(mesh):
    placed = (P("samp", None), P("samp", "boot"), P(), P(), P())
    return jax.shard_map(
        shards, mesh=mesh, in_specs=placed, out_specs=P("samp", "boot"), check_vma=False
    )
```

profile of v0, /device:TPU:0, one launch (start us, length us, event | category | flops | bytes accessed | tf_op | source)
XLA Modules:
  0.0 128.8 jit_solution(401770869329293279)
XLA Ops:
  6.5 0.0 copy-start
  6.5 0.0 all-reduce.3.cloned.1.call-start
  6.6 0.9 select_reduce_fusion
  7.5 0.8 copy-done
  8.3 0.0 copy-start.3
  8.3 4.5 %convolution_multiply_fusion = f32[512,640]{1,0:T(8,128)} fusion(bf16[2024,512]{1,0:T(8,128)(2,1)} %param.5, bf16[2024,640]{1,0:T(8,128)(2,1)S(1)} %copy-done, f32[512]{0:T(512)S(1)} %broadcast_multiply_fusion.1), kind=kOutput, calls=%fused_computation.4 | convolution fusion | flops 1326776320 | bytes 5976064 | tf_op jit(solution)/shard_map/dot_general | solution.py:23
  12.8 0.0 all-reduce.3.cloned.1.call-update
  12.8 0.0 copy-start.2
  12.8 0.0 copy-done.3
  12.9 0.1 dynamic_slice.3
  12.9 96.9 %all-reduce.3.cloned.1.call-done = f32[512,640]{1,0:T(8,128)} async-done(((f32[512,640]{1,0:T(8,128)}), f32[512,640]{1,0:T(8,128)}) %all-reduce.3.cloned.1.call-update) | async-done | bytes 1310736 | tf_op jit(solution)/shard_map/psum | solution.py:33
  109.8 0.0 copy-start.1
  109.8 1.9 %mul.96 = f32[512,640]{1,0:T(8,128)S(1)} multiply(f32[512,640]{1,0:T(8,128)} %all-reduce.3.cloned.1.call-done, f32[512,640]{1,0:T(8,128)} %all-reduce.3.cloned.1.call-done) | non-fusion elementwise | flops 327680 | bytes 3932160 | tf_op jit(solution)/shard_map/mul | solution.py:36
  111.7 0.0 copy-done.2
  111.8 0.1 copy-done.1
  111.9 1.0 fusion
  112.9 0.2 fusion.5
  113.1 8.1 %all-reduce = (f32[2,11]{0,1:T(8,128)S(1)}, f32[2,11]{0,1:T(8,128)S(1)}) all-reduce(f32[2,11]{0,1:T(8,128)S(1)} %get-tuple-element.6, f32[2,11]{0,1:T(8,128)S(1)} %get-tuple-element.5), channel_id=1, replica_groups=mesh['boot'=2,'samp'=16] {'boot'}, use_global_device_ids=true, to_apply=%region_5.6 | all-reduce | flops 44 | bytes 352 | tf_op jit(solution)/shard_map/psum | solution.py:48
  121.2 0.7 fusion.4
  (5 shorter events, 0.1 us)
Async XLA Ops:
  6.5 1.7 %copy-start = (bf16[2024,640]{1,0:T(8,128)(2,1)S(1)}, bf16[2024,640]{1,0:T(8,128)(2,1)}, u32[]{:S(2)}) copy-start(bf16[2024,640]{1,0:T(8,128)(2,1)} %param.6) | copy-start | bytes 7772164
  6.5 103.3 %all-reduce.3.cloned.1.call-start = ((), (), s32[]{:S(2)}) async-start(), calls=%async_computation | async-start | bytes 2621440 | tf_op jit(solution)/shard_map/psum | solution.py:33
  8.3 4.6 %copy-start.3 = (s32[32]{0:T(128)S(1)}, s32[32]{0:T(128)}, u32[]{:S(2)}) copy-start(s32[32]{0:T(128)} %param.9) | copy-start | bytes 388
  12.8 98.9 %copy-start.2 = (s32[512]{0:T(512)S(1)}, s32[512]{0:T(512)}, u32[]{:S(2)}) copy-start(s32[512]{0:T(512)} %param.8) | copy-start | bytes 6148
  109.8 2.1 %copy-start.1 = (f32[512,640]{1,0:T(8,128)S(1)}, f32[512,640]{1,0:T(8,128)}, u32[]{:S(2)}) copy-start(f32[512,640]{1,0:T(8,128)} %all-reduce.3.cloned.1.call-done) | copy-start | bytes 3932164
Sparse Core Ops, SparseCore 0:
  12.9 96.7 all-reduce.2
where the time goes:
time: 129 us
  waiting for transfers between devices  96.9 us (75%)
  between operations  13.4 us (10%)
  blocking collectives  8.14 us (6%)
  matrix products  5.49 us (4%)
  other arithmetic  3.86 us (3%)
    psum x1, waiting for transfers between devices, shards(): scores = lax.psum(partial_value, 'samp')  96.9 us
    psum x1, blocking collectives, shards(): lax.psum((jnp.sum(mixtures, axis=2), jnp.sum(mixtures * mixtures, axis=2)...  8.14 us
    dot_general x1, matrix products, sample_product(): lax.dot_general(dose_part, residuals, (((0,), (0,)), ((), ())), preferred...  4.52 us
  transfers between devices with their start and end apart: 1, of which 1 were waited for; matrix products, arithmetic and copies ran while one was open for 0% of the time, Pallas kernels for 0%

commit v1 on v0

--- a/solution.py
+++ b/solution.py
@@ -30,7 +30,10 @@
     scaling = variant_weights(maf_bin) / math.sqrt(sample_total)
     my_index = lax.axis_index("samp")
     partial_value = sample_product(dosage, residuals) * scaling[:, None]
-    scores = lax.psum(partial_value, "samp")
+    devs = lax.axis_size("samp")
+    scores = partial_value
+    for ii in [to_i for to_i in (1, 2, 4, 8, 16) if to_i < devs]:
+        scores = scores + lax.ppermute(scores, "samp", [(m, m ^ ii) for m in range(devs)])
     owned_genes = lax.dynamic_slice_in_dim(gene_order, my_index * GENE_DEV, GENE_DEV)
     member = (owned_genes[:, None] == gene_map[None, :]).astype(jnp.float32)
     stacked = jnp.concatenate([scores, scores * scores], axis=1)

time: 129 us -> 143 us (1.11)
  waiting for transfers between devices: 96.9 us -> 116 us
  between operations: 13.4 us -> 0.05 us
  starting transfers between devices: 0.01 us -> 7.89 us
    ppermute x0 -> x4, waiting for transfers between devices: none -> 116 us  [shards(): lax.ppermute(scores, 'samp', [(m, m ^ ii) for m in range(devs)])]
    psum x1 -> x0, waiting for transfers between devices: 96.9 us -> none  [shards(): scores = lax.psum(partial_value, 'samp')]
    ppermute x0 -> x4, starting transfers between devices: none -> 7.89 us  [shards(): lax.ppermute(scores, 'samp', [(m, m ^ ii) for m in range(devs)])]
    add x0 -> x3, other arithmetic: none -> 1.46 us  [shards(): scores + lax.ppermute(scores, 'samp', [(m, m ^ ii) for m in range(devs)])]
  transfers between devices with their start and end apart: 1 -> 4, of which waited for: 1 -> 4; matrix products, arithmetic and copies ran while one was open for 0% -> 0% of each run, Pallas kernels for 0% -> 0%
where the time goes in v1:
time: 143 us
  waiting for transfers between devices  116 us (81%)
  starting transfers between devices  7.89 us (6%)
  blocking collectives  7.83 us (5%)
  other arithmetic  5.25 us (4%)
  matrix products  4.39 us (3%)
    ppermute x4, waiting for transfers between devices, shards(): lax.ppermute(scores, 'samp', [(m, m ^ ii) for m in range(devs)])  116 us
    ppermute x4, starting transfers between devices, shards(): lax.ppermute(scores, 'samp', [(m, m ^ ii) for m in range(devs)])  7.89 us
    psum x1, blocking collectives, shards(): lax.psum((jnp.sum(mixtures, axis=2), jnp.sum(mixtures * mixtures, axis=2)...  7.83 us
    dot_general x1, matrix products, sample_product(): lax.dot_general(dose_part, residuals, (((0,), (0,)), ((), ())), preferred...  3.43 us
  transfers between devices with their start and end apart: 4, of which 4 were waited for; matrix products, arithmetic and copies ran while one was open for 0% of the time, Pallas kernels for 0%

profile of v1, /device:TPU:0, one launch (start us, length us, event | category | flops | bytes accessed | tf_op | source)
XLA Modules:
  0.0 142.6 jit_solution(15410449317402304512)
XLA Ops:
  0.0 0.0 copy-start
  0.0 0.9 select_reduce_fusion
  1.0 0.8 copy-done
  1.7 3.4 %convolution_multiply_fusion = f32[512,640]{1,0:T(8,128)S(1)} fusion(bf16[2024,512]{1,0:T(8,128)(2,1)} %param.5, bf16[2024,640]{1,0:T(8,128)(2,1)S(1)} %copy-done, f32[512]{0:T(512)S(1)} %broadcast_multiply_fusion.1), kind=kOutput, calls=%fused_computation.4 | convolution fusion | flops 1326776320 | bytes 5976064 | tf_op jit(solution)/shard_map/dot_general | solution.py:23
  5.2 0.6 collective-permute-start
  5.7 2.7 %collective-permute-done = f32[512,640]{1,0:T(8,128)S(1)} collective-permute-done((f32[512,640]{1,0:T(8,128)S(1)}, f32[512,640]{1,0:T(8,128)S(1)}, u32[]{:S(2)}, u32[]{:S(2)}) %collective-permute-start) | collective-permute-done | bytes 1310752 | tf_op jit(solution)/shard_map/ppermute | solution.py:36
  8.4 0.1 add.39
  8.5 2.9 %collective-permute-start.1 = (f32[512,640]{1,0:T(8,128)S(1)}, f32[512,640]{1,0:T(8,128)S(1)}, u32[]{:S(2)}, u32[]{:S(2)}) collective-permute-start(f32[512,640]{1,0:T(8,128)S(1)} %add.39), channel_id=1, source_target_pairs={{0,2},{1,3},{2,0},{3,1},{4,6},{5,7},{6,4},{7,5},{8,10},{9,11},{10,... | collective-permute-start | bytes 3932168 | tf_op jit(solution)/shard_map/ppermute | solution.py:36
  11.5 29.1 %collective-permute-done.1 = f32[512,640]{1,0:T(8,128)S(1)} collective-permute-done((f32[512,640]{1,0:T(8,128)S(1)}, f32[512,640]{1,0:T(8,128)S(1)}, u32[]{:S(2)}, u32[]{:S(2)}) %collective-permute-start.1) | collective-permute-done | bytes 1310752 | tf_op jit(solution)/shard_map/ppermute | solution.py:36
  40.6 0.1 add.40
  40.7 0.0 copy-start.2
  40.7 1.9 %collective-permute-start.2 = (f32[512,640]{1,0:T(8,128)S(1)}, f32[512,640]{1,0:T(8,128)S(1)}, u32[]{:S(2)}, u32[]{:S(2)}) collective-permute-start(f32[512,640]{1,0:T(8,128)S(1)} %add.40), channel_id=1, source_target_pairs={{0,4},{1,5},{2,6},{3,7},{4,0},{5,1},{6,2},{7,3},{8,12},{9,13},{10,... | collective-permute-start | bytes 3932168 | tf_op jit(solution)/shard_map/ppermute | solution.py:36
  42.6 28.4 %collective-permute-done.2 = f32[512,640]{1,0:T(8,128)S(1)} collective-permute-done((f32[512,640]{1,0:T(8,128)S(1)}, f32[512,640]{1,0:T(8,128)S(1)}, u32[]{:S(2)}, u32[]{:S(2)}) %collective-permute-start.2) | collective-permute-done | bytes 1310752 | tf_op jit(solution)/shard_map/ppermute | solution.py:36
  71.0 1.2 add.41
  72.2 2.5 %collective-permute-start.3 = (f32[512,640]{1,0:T(8,128)}, f32[512,640]{1,0:T(8,128)}, u32[]{:S(2)}, u32[]{:S(2)}) collective-permute-start(f32[512,640]{1,0:T(8,128)} %add.41), channel_id=1, source_target_pairs={{0,8},{1,9},{2,10},{3,11},{4,12},{5,13},{6,14},{7,15},{8,0},{9,1},... | collective-permute-start | bytes 3932168 | tf_op jit(solution)/shard_map/ppermute | solution.py:36
  74.7 0.0 copy-done.2
  74.7 0.1 dynamic_slice.3
  74.8 0.0 copy-start.1
  74.8 56.1 %collective-permute-done.3 = f32[512,640]{1,0:T(8,128)} collective-permute-done((f32[512,640]{1,0:T(8,128)}, f32[512,640]{1,0:T(8,128)}, u32[]{:S(2)}, u32[]{:S(2)}) %collective-permute-start.3) | collective-permute-done | bytes 1310752 | tf_op jit(solution)/shard_map/ppermute | solution.py:36
  130.9 1.9 %fusion.10 = (f32[512,640]{1,0:T(8,128)S(1)}, f32[512,640]{1,0:T(8,128)S(1)}) fusion(f32[512,640]{1,0:T(8,128)} %add.41, f32[512,640]{1,0:T(8,128)} %collective-permute-done.3), kind=kLoop, calls=%fused_computation.23 | loop fusion | flops 655360 | bytes 5242880 | tf_op jit(solution)/shard_map/mul | solution.py:39
  132.8 0.0 copy-done.1
  132.8 1.0 fusion
  133.8 0.2 fusion.5
  134.0 7.8 %all-reduce = (f32[2,11]{0,1:T(8,128)S(1)}, f32[2,11]{0,1:T(8,128)S(1)}) all-reduce(f32[2,11]{0,1:T(8,128)S(1)} %get-tuple-element.6, f32[2,11]{0,1:T(8,128)S(1)} %get-tuple-element.5), channel_id=1, replica_groups=mesh['boot'=2,'samp'=16] {'boot'}, use_global_device_ids=true, to_apply=%region_4.5 | all-reduce | flops 44 | bytes 352 | tf_op jit(solution)/shard_map/psum | solution.py:51
  141.8 0.7 fusion.4
  (5 shorter events, 0.1 us)
Async XLA Ops:
  0.0 1.7 %copy-start = (bf16[2024,640]{1,0:T(8,128)(2,1)S(1)}, bf16[2024,640]{1,0:T(8,128)(2,1)}, u32[]{:S(2)}) copy-start(bf16[2024,640]{1,0:T(8,128)(2,1)} %param.6) | copy-start | bytes 7772164
  5.2 3.2 %collective-permute-start = (f32[512,640]{1,0:T(8,128)S(1)}, f32[512,640]{1,0:T(8,128)S(1)}, u32[]{:S(2)}, u32[]{:S(2)}) collective-permute-start(f32[512,640]{1,0:T(8,128)S(1)} %convolution_multiply_fusion), channel_id=1, source_target_pairs={{0,1},{1,0},{2,3},{3,2},{4,5},{5,4},{6,7},{7,6},{8,9},{9,8},{10,11... | collective-permute-start | bytes 3932168 | tf_op jit(solution)/shard_map/ppermute | solution.py:36
  8.5 32.0 %collective-permute-start.1 = (f32[512,640]{1,0:T(8,128)S(1)}, f32[512,640]{1,0:T(8,128)S(1)}, u32[]{:S(2)}, u32[]{:S(2)}) collective-permute-start(f32[512,640]{1,0:T(8,128)S(1)} %add.39), channel_id=1, source_target_pairs={{0,2},{1,3},{2,0},{3,1},{4,6},{5,7},{6,4},{7,5},{8,10},{9,11},{10,... | collective-permute-start | bytes 3932168 | tf_op jit(solution)/shard_map/ppermute | solution.py:36
  40.7 34.0 %copy-start.2 = (s32[32]{0:T(128)S(1)}, s32[32]{0:T(128)}, u32[]{:S(2)}) copy-start(s32[32]{0:T(128)} %param.9) | copy-start | bytes 388
  40.7 30.3 %collective-permute-start.2 = (f32[512,640]{1,0:T(8,128)S(1)}, f32[512,640]{1,0:T(8,128)S(1)}, u32[]{:S(2)}, u32[]{:S(2)}) collective-permute-start(f32[512,640]{1,0:T(8,128)S(1)} %add.40), channel_id=1, source_target_pairs={{0,4},{1,5},{2,6},{3,7},{4,0},{5,1},{6,2},{7,3},{8,12},{9,13},{10,... | collective-permute-start | bytes 3932168 | tf_op jit(solution)/shard_map/ppermute | solution.py:36
  72.2 58.7 %collective-permute-start.3 = (f32[512,640]{1,0:T(8,128)}, f32[512,640]{1,0:T(8,128)}, u32[]{:S(2)}, u32[]{:S(2)}) collective-permute-start(f32[512,640]{1,0:T(8,128)} %add.41), channel_id=1, source_target_pairs={{0,8},{1,9},{2,10},{3,11},{4,12},{5,13},{6,14},{7,15},{8,0},{9,1},... | collective-permute-start | bytes 3932168 | tf_op jit(solution)/shard_map/ppermute | solution.py:36
  74.8 58.0 %copy-start.1 = (s32[512]{0:T(512)S(1)}, s32[512]{0:T(512)}, u32[]{:S(2)}) copy-start(s32[512]{0:T(512)} %param.8) | copy-start | bytes 6148
